TPU v7x, 256 devices: a whole 4x4x8 slice. The times are simulated.
256 devices in a mesh: mon: 64 (over y, z, core), out: 4 (over x).
Axes of the slice: x: 4, y: 4, z: 8, core: 2. Of those that a mesh axis runs over, the one named last changes fastest.
Arguments:
- mon_flow: bfloat16 [24576, 128], P('mon'), may hold values from -2.5 to 2.5
- out_flow: bfloat16 [4, 4096, 128], P('out', 'mon'), may hold values from -2.5 to 2.5
- rating: float32 [24576], P('mon'), may hold values from 1 to 3
- weights: float32 [128], replicated, may hold values from 0.25 to 1
- lodf: bfloat16 [64, 4, 8, 128, 128], P('mon', 'out'), may hold values from -1 to 1
- tile_mon: int32 [64, 4, 8], P('mon', 'out'), may hold values from 0 to 2
- tile_out: int32 [64, 4, 8], P('mon', 'out'), may hold values from 0 to 31
- tile_count: int32 [64, 4], P('mon', 'out'), may hold values from 1 to 8, as said below
Outputs:
- grad_mon: float32 [24576, 128], P(('mon', 'out'))
- grad_out: float32 [4, 4096, 128], P('out', 'mon')
Inputs may be any that keep to these rules, and one draw needn't show every extreme that they name: `tile_count`: each device has 1 to 8 live slots; some device has exactly 8 in every draw.
All inputs are finite; a program needn't handle non-finite values.
Results may differ from a plain program's by a relative error of at most 0.00085.
Values may be sent and summed in bfloat16 or wider, within the bound.
A program may use at most 64 MiB of HBM per device.

v0:
```python
import jax
import jax.numpy as jnp
from jax import lax
from jax.sharding import PartitionSpec as P


def tile_grads(lodf_tile, mon_block, out_block, rating_rows, weights):
    coupling = lodf_tile.astype(jnp.float32)
    post_flow = (
        mon_block.astype(jnp.float32)[:, None, :]
        + coupling[:, :, None] * out_block.astype(jnp.float32)[None, :, :]
    )
    inverse = 1.0 / (rating_rows * rating_rows)
    excess = post_flow * post_flow * inverse[:, None, None] - 1.0
    derivative = jax.nn.softplus(excess) * jax.nn.sigmoid(excess) * post_flow
    derivative = (
        derivative * (4.0 / coupling.shape[0]) * inverse[:, None, None] * weights[None, None, :]
    )
    return (jnp.sum(derivative, axis=1), jnp.sum(coupling[:, :, None] * derivative, axis=0))


def local(mon_flow, out_flow, rating, weights, lodf, tile_mon, tile_out, tile_count):
    width = lodf.shape[-1]
    scen = mon_flow.shape[1]
    gathered = lax.all_gather(out_flow, "mon", axis=1, tiled=True)[0]
    outage_blocks = gathered.reshape(-1, width, scen)
    mon_start = jnp.zeros(mon_flow.shape, jnp.float32)
    out_start = jnp.zeros(outage_blocks.shape, jnp.float32)

    def one_tile(mon_part, lodf_tile, mon_index, out_block):
        start = mon_index * width
        mon_rows = lax.dynamic_slice_in_dim(mon_flow, start, width, 0)
        rating_rows = lax.dynamic_slice_in_dim(rating, start, width, 0)
        grad_m, grad_k = tile_grads(lodf_tile, mon_rows, out_block, rating_rows, weights)
        old_rows = lax.dynamic_slice_in_dim(mon_part, start, width, 0)
        return (lax.dynamic_update_slice_in_dim(mon_part, old_rows + grad_m, start, 0), grad_k)

    def own_tile(slot_index, totals):
        mon_part, out_part = totals
        out_index = tile_out[0, 0, slot_index]
        mon_part, grad_k = one_tile(
            mon_part, lodf[0, 0, slot_index], tile_mon[0, 0, slot_index], outage_blocks[out_index]
        )
        old_block = lax.dynamic_index_in_dim(out_part, out_index, 0, keepdims=False)
        out_part = lax.dynamic_update_index_in_dim(out_part, old_block + grad_k, out_index, 0)
        return (mon_part, out_part)

    own_count = tile_count[0, 0]
    mon_part, out_part = lax.fori_loop(0, own_count, own_tile, (mon_start, out_start))
    grad_mon = lax.psum_scatter(mon_part, "out", scatter_dimension=0, tiled=True)
    grad_out = lax.psum_scatter(
        out_part.reshape(1, -1, scen), "mon", scatter_dimension=1, tiled=True
    )
    return (grad_mon, grad_out)


def solution(mesh):
    in_specs = (
        P("mon", None),
        P("out", "mon", None),
        P("mon"),
        P(),
        P("mon", "out", None, None, None),
        P("mon", "out", None),
        P("mon", "out", None),
        P("mon", "out"),
    )
    out_specs = (P(("mon", "out"), None), P("out", "mon", None))
    return jax.shard_map(local, mesh=mesh, in_specs=in_specs, out_specs=out_specs, check_vma=False)
```

profile of v0, /device:TPU:4, one launch (start us, length us, event | category | flops | bytes accessed | tf_op | source)
XLA Modules:
  0.0 414.8 jit_solution(17934352737875300077)
XLA Ops:
  7.2 0.0 copy-start.3
  7.2 0.0 copy-start.2
  7.2 0.0 copy-start.4
  7.2 0.0 all-gather.2.cloned.1.call-start
  7.2 0.7 all-gather.2.cloned.1.call-update
  7.9 0.0 reduce-scatter.3.cloned.1.call-start
  8.0 82.2 %all-gather.2.cloned.1.call-done = bf16[1,4096,128]{2,1,0:T(8,128)(2,1)} async-done(((bf16[1,64,128]{2,1,0:T(8,128)(2,1)}), bf16[1,4096,128]{2,1,0:T(8,128)(2,1)}) %all-gather.2.cloned.1.call-update) | async-done | bytes 1048592 | tf_op jit(solution)/shard_map/all_gather | solution.py:25
  90.2 0.2 broadcast_in_dim.6
  90.4 0.0 copy-done.3
  90.4 0.0 copy-done.2
  90.4 0.0 copy-done.4
  90.4 57.0 %while.14 = (s32[]{:T(128)}, f32[384,128]{1,0:T(8,128)S(1)}, f32[32,128,128]{2,1,0:T(8,128)S(1)}, s32[]{:T(128)}, s32[1,1,8]{2,1,0:T(1,128)S(1)}, /*index=5*/bf1...) while((s32[]{:T(128)}, f32[384,128]{1,0:T(8,128)S(1)}, ...), condition=%wide.region_3.4_spmd, body=%wide.region_0.3_spmd.sunk | while | flops 44089740 | bytes 1019183 | solution.py:49
  91.1 0.6 constant_dynamic-slice_fusion.3
  95.6 0.8 broadcast_multiply_fusion.2
  96.3 0.8 bitcast_convert_fusion.4
  97.1 0.8 dynamic-slice_convert_fusion.2
  97.9 0.8 bitcast_convert_fusion.5
  98.6 10.5 %multiply_reduce_fusion.2 = (f32[128,128]{1,0:T(8,128)S(1)}, f32[128,128]{1,0:T(8,128)S(1)}) fusion(f32[128,128]{1,0:T(8,128)S(1)} %bitcast_convert_fusion.4, f32[128]{0:T(128)S(1)} %get-tuple-element.295, f32[128]{0:T(128)S(1)} %get-tuple-element.248, f32[128]{0:T(128)S(1)} %get-tuple-element.249, f32[128,128]{1,0:T(8,128)S(1)} %bitcast_convert_fusion.5, ...), kind=kLoop, calls=%fused_computation.5.clone.1 | loop fusion | flops 44007424 | bytes 329216 | tf_op jit(solution)/shard_map/while/body/reduce_sum | solution.py:19
  109.9 0.6 constant_dynamic-slice_fusion.3
  114.4 0.8 broadcast_multiply_fusion.2
  115.1 0.8 bitcast_convert_fusion.4
  115.9 0.8 dynamic-slice_convert_fusion.2
  116.6 0.8 bitcast_convert_fusion.5
  117.4 10.5 %multiply_reduce_fusion.2 = (f32[128,128]{1,0:T(8,128)S(1)}, f32[128,128]{1,0:T(8,128)S(1)}) fusion(f32[128,128]{1,0:T(8,128)S(1)} %bitcast_convert_fusion.4, f32[128]{0:T(128)S(1)} %get-tuple-element.295, f32[128]{0:T(128)S(1)} %get-tuple-element.248, f32[128]{0:T(128)S(1)} %get-tuple-element.249, f32[128,128]{1,0:T(8,128)S(1)} %bitcast_convert_fusion.5, ...), kind=kLoop, calls=%fused_computation.5.clone.1 | loop fusion | flops 44007424 | bytes 329216 | tf_op jit(solution)/shard_map/while/body/reduce_sum | solution.py:19
  128.7 0.6 constant_dynamic-slice_fusion.3
  133.1 0.8 broadcast_multiply_fusion.2
  133.9 0.8 bitcast_convert_fusion.4
  134.7 0.8 dynamic-slice_convert_fusion.2
  135.4 0.8 bitcast_convert_fusion.5
  136.2 10.5 %multiply_reduce_fusion.2 = (f32[128,128]{1,0:T(8,128)S(1)}, f32[128,128]{1,0:T(8,128)S(1)}) fusion(f32[128,128]{1,0:T(8,128)S(1)} %bitcast_convert_fusion.4, f32[128]{0:T(128)S(1)} %get-tuple-element.295, f32[128]{0:T(128)S(1)} %get-tuple-element.248, f32[128]{0:T(128)S(1)} %get-tuple-element.249, f32[128,128]{1,0:T(8,128)S(1)} %bitcast_convert_fusion.5, ...), kind=kLoop, calls=%fused_computation.5.clone.1 | loop fusion | flops 44007424 | bytes 329216 | tf_op jit(solution)/shard_map/while/body/reduce_sum | solution.py:19
  147.5 0.0 copy-start.1
  147.5 0.0 copy-start
  147.5 0.6 copy-done.1
  148.1 0.0 reduce-scatter.3.cloned.1.call-update
  148.1 0.0 reduce-scatter.5.cloned.1.call-start
  148.2 0.7 copy-done
  148.9 0.0 reduce-scatter.5.cloned.1.call-update
  148.9 112.1 %reduce-scatter.3.cloned.1.call-done = f32[96,128]{1,0:T(8,128)} async-done(((f32[384,128]{1,0:T(8,128)}), f32[96,128]{1,0:T(8,128)}) %reduce-scatter.3.cloned.1.call-update) | async-done | bytes 49168 | tf_op jit(solution)/shard_map/reduce_scatter | solution.py:50
  261.0 147.2 %reduce-scatter.5.cloned.1.call-done = f32[1,64,128]{2,1,0:T(8,128)} async-done(((f32[1,4096,128]{2,1,0:T(8,128)}), f32[1,64,128]{2,1,0:T(8,128)}) %reduce-scatter.5.cloned.1.call-update) | async-done | bytes 32784 | tf_op jit(solution)/shard_map/reduce_scatter | solution.py:51
  (7 shorter events, 0.1 us)
Async XLA Ops:
  7.2 83.2 %copy-start.3 = (s32[1,1,8]{2,1,0:T(1,128)S(1)}, s32[1,1,8]{2,1,0:T(1,128)}, u32[]{:S(2)}) copy-start(s32[1,1,8]{2,1,0:T(1,128)} %param.16) | copy-start | bytes 100
  7.2 83.2 %copy-start.2 = (s32[1,1,8]{2,1,0:T(1,128)S(1)}, s32[1,1,8]{2,1,0:T(1,128)}, u32[]{:S(2)}) copy-start(s32[1,1,8]{2,1,0:T(1,128)} %param.15) | copy-start | bytes 100
  7.2 83.2 %copy-start.4 = (f32[128]{0:T(128)S(1)}, f32[128]{0:T(128)}, u32[]{:S(2)}) copy-start(f32[128]{0:T(128)} %param.13) | copy-start | bytes 1540
  7.2 83.0 %all-gather.2.cloned.1.call-start = ((), (), s32[]{:S(2)}) async-start(), calls=%async_computation.2 | async-start | bytes 1064960 | tf_op jit(solution)/shard_map/all_gather | solution.py:25
  7.9 253.1 %reduce-scatter.3.cloned.1.call-start = ((), (), s32[]{:S(2)}) async-start(), calls=%async_computation.3 | async-start | bytes 245760 | tf_op jit(solution)/shard_map/reduce_scatter | solution.py:50
  147.5 0.7 copy-start.1
  147.5 1.4 copy-start
  148.1 260.1 %reduce-scatter.5.cloned.1.call-start = ((), (), s32[]{:S(2)}) async-start(), calls=%async_computation.4 | async-start | bytes 2129920 | tf_op jit(solution)/shard_map/reduce_scatter | solution.py:51
Sparse Core Ops, SparseCore 0:
  10.8 79.3 all-gather.1
  148.3 112.7 reduce-scatter.2
  266.2 142.0 reduce-scatter.4
where the time goes:
time: 417 us; the launch traced here: 415 us
  waiting for transfers between devices  342 us (82%)
  other arithmetic  42.7 us (10%)
  loops' own time  14.3 us (3%)
  between operations  13.8 us (3%)
    reduce_scatter x1, waiting for transfers between devices, local(): lax.psum_scatter(out_part.reshape(1, -1, scen), 'mon', scatter_dimension=...  147 us
    reduce_scatter x1, waiting for transfers between devices, local(): lax.psum_scatter(mon_part, 'out', scatter_dimension=0, tiled=True)  112 us
    all_gather x1, waiting for transfers between devices, local(): gathered = lax.all_gather(out_flow, 'mon', axis=1, tiled=True)[0]  82.2 us
    reduce_sum x3, other arithmetic, tile_grads(): jnp.sum(coupling[:, :, None] * derivative, axis=0)  31.6 us
    another operation x1, loops' own time, local(): lax.fori_loop(0, own_count, own_tile, (mon_start, out_start))  14.3 us
  transfers between devices with their start and end apart: 3, of which 3 were waited for; matrix products, arithmetic and copies ran while one was open for 0% of the time, Pallas kernels for 0%

commit v1 on v0

--- a/solution.py
+++ b/solution.py
@@ -1,7 +1,21 @@
+import functools
 import jax
 import jax.numpy as jnp
 from jax import lax
 from jax.sharding import PartitionSpec as P
+
+
+def proceed_tokens(packet, row_dim):
+    nodes = []
+    for _ in range(jax.lax.psum(1, axis_name="mon")):
+        nodes.append(packet)
+    return jnp.concatenate(
+        jax.lax.all_to_all(jnp.stack(nodes, axis=0), split_axis=0, concat_axis=0, axis_name="mon"),
+        row_dim,
+    )
+
+
+pack_lanes = functools.partial(proceed_tokens, row_dim=1)
 
 
 def tile_grads(lodf_tile, mon_block, out_block, rating_rows, weights):
@@ -22,7 +36,7 @@
 def local(mon_flow, out_flow, rating, weights, lodf, tile_mon, tile_out, tile_count):
     width = lodf.shape[-1]
     scen = mon_flow.shape[1]
-    gathered = lax.all_gather(out_flow, "mon", axis=1, tiled=True)[0]
+    gathered = pack_lanes(out_flow)[0]
     outage_blocks = gathered.reshape(-1, width, scen)
     mon_start = jnp.zeros(mon_flow.shape, jnp.float32)
     out_start = jnp.zeros(outage_blocks.shape, jnp.float32)

time: 417 us -> 367 us (0.88)
  waiting for transfers between devices: 342 us -> 281 us
  starting transfers between devices: 0.12 us -> 12.3 us
    all_gather x1 -> x0, waiting for transfers between devices: 82.2 us -> none  [local(): gathered = lax.all_gather(out_flow, 'mon', axis=1, tiled=True)[0]]
    all_to_all x0 -> x1, waiting for transfers between devices: none -> 28.1 us  [proceed_tokens(): jax.lax.all_to_all(jnp.stack(nodes, axis=0), split_axis=0, concat_axis=0,...]
    all_to_all x0 -> x1, starting transfers between devices: none -> 12.2 us  [proceed_tokens(): jax.lax.all_to_all(jnp.stack(nodes, axis=0), split_axis=0, concat_axis=0,...]
    reduce_scatter x1, waiting for transfers between devices: 112 us -> 106 us  [local(): lax.psum_scatter(mon_part, 'out', scatter_dimension=0, tiled=True)]
where the time goes in v1:
time: 367 us; the launch traced here: 365 us
  waiting for transfers between devices  281 us (77%)
  other arithmetic  40.4 us (11%)
  between operations  14.1 us (4%)
  loops' own time  13.6 us (4%)
  starting transfers between devices  12.3 us (3%)
    reduce_scatter x1, waiting for transfers between devices, local(): lax.psum_scatter(out_part.reshape(1, -1, scen), 'mon', scatter_dimension=...  147 us
    reduce_scatter x1, waiting for transfers between devices, local(): lax.psum_scatter(mon_part, 'out', scatter_dimension=0, tiled=True)  106 us
    reduce_sum x3, other arithmetic, tile_grads(): jnp.sum(coupling[:, :, None] * derivative, axis=0)  31.7 us
    all_to_all x1, waiting for transfers between devices, proceed_tokens(): jax.lax.all_to_all(jnp.stack(nodes, axis=0), split_axis=0, concat_axis=0,...  28.1 us
    another operation x1, loops' own time, local(): lax.fori_loop(0, own_count, own_tile, (mon_start, out_start))  13.6 us
    all_to_all x1, starting transfers between devices, proceed_tokens(): jax.lax.all_to_all(jnp.stack(nodes, axis=0), split_axis=0, concat_axis=0,...  12.2 us
  transfers between devices with their start and end apart: 3, of which 3 were waited for; matrix products, arithmetic and copies ran while one was open for 0% of the time, Pallas kernels for 0%

profile of v1, /device:TPU:4, one launch (start us, length us, event | category | flops | bytes accessed | tf_op | source)
XLA Modules:
  0.0 365.4 jit_solution(6838186443128524246)
XLA Ops:
  7.2 1.9 stack.2
  9.1 0.0 copy-start.2
  9.1 0.0 copy-start.3
  9.1 0.0 copy-start.4
  9.1 12.2 %all-to-all-start = ((bf16[64,1,64,128]{3,2,1,0:T(8,128)(2,1)}), bf16[64,1,64,128]{3,2,1,0:T(8,128)(2,1)S(1)}, u32[]{:S(2)}, u32[]{:S(2)}) async-start(bf16[64,1,64,128]{3,2,1,0:T(8,128)(2,1)} %stack.2), calls=%async_computation | async-start | bytes 2097152 | tf_op jit(solution)/shard_map/all_to_all | solution.py:13
  21.4 0.0 reduce-scatter.3.cloned.1.call-start
  21.4 28.1 %all-to-all-done = bf16[64,1,64,128]{3,2,1,0:T(8,128)(2,1)S(1)} async-done(((bf16[64,1,64,128]{3,2,1,0:T(8,128)(2,1)}), bf16[64,1,64,128]{3,2,1,0:T(8,128)(2,1)S(1)}, u32[]{:S(2)}, u32[]{:S(2)}) %all-to-all-start) | async-done | bytes 1048608 | tf_op jit(solution)/shard_map/all_to_all | solution.py:13
  49.6 0.2 broadcast_in_dim.6
  49.8 0.0 copy-done.2
  49.8 0.0 copy-done.3
  49.8 0.0 copy-done.4
  49.8 54.0 %while.14 = (s32[]{:T(128)}, f32[384,128]{1,0:T(8,128)S(1)}, f32[32,128,128]{2,1,0:T(8,128)S(1)}, s32[]{:T(128)}, s32[1,1,8]{2,1,0:T(1,128)S(1)}, /*index=5*/bf1...) while((s32[]{:T(128)}, f32[384,128]{1,0:T(8,128)S(1)}, ...), condition=%wide.region_3.4_spmd, body=%wide.region_0.3_spmd.sunk | while | flops 44089740 | bytes 1019183 | solution.py:63
  50.5 0.6 constant_dynamic-slice_fusion.3
  54.7 0.8 broadcast_multiply_fusion.2
  55.5 0.8 bitcast_convert_fusion.4
  56.2 0.8 dynamic-slice_convert_fusion.2
  57.0 10.6 %multiply_reduce_fusion.2 = (f32[128,128]{1,0:T(8,128)S(1)}, f32[128,128]{1,0:T(8,128)S(1)}) fusion(f32[128,128]{1,0:T(8,128)S(1)} %bitcast_convert_fusion.4, f32[128]{0:T(128)S(1)} %get-tuple-element.295, f32[128]{0:T(128)S(1)} %get-tuple-element.248, f32[128]{0:T(128)S(1)} %get-tuple-element.249, f32[128,128]{1,0:T(8,128)S(1)} %bitcast_convert_fusion.5, ...), kind=kLoop, calls=%fused_computation.5.clone.1 | loop fusion | flops 44007424 | bytes 329216 | tf_op jit(solution)/shard_map/while/body/reduce_sum | solution.py:33
  68.3 0.6 constant_dynamic-slice_fusion.3
  72.5 0.8 broadcast_multiply_fusion.2
  73.3 0.8 bitcast_convert_fusion.4
  74.0 0.8 dynamic-slice_convert_fusion.2
  74.8 10.6 %multiply_reduce_fusion.2 = (f32[128,128]{1,0:T(8,128)S(1)}, f32[128,128]{1,0:T(8,128)S(1)}) fusion(f32[128,128]{1,0:T(8,128)S(1)} %bitcast_convert_fusion.4, f32[128]{0:T(128)S(1)} %get-tuple-element.295, f32[128]{0:T(128)S(1)} %get-tuple-element.248, f32[128]{0:T(128)S(1)} %get-tuple-element.249, f32[128,128]{1,0:T(8,128)S(1)} %bitcast_convert_fusion.5, ...), kind=kLoop, calls=%fused_computation.5.clone.1 | loop fusion | flops 44007424 | bytes 329216 | tf_op jit(solution)/shard_map/while/body/reduce_sum | solution.py:33
  86.1 0.6 constant_dynamic-slice_fusion.3
  90.3 0.8 broadcast_multiply_fusion.2
  91.1 0.8 bitcast_convert_fusion.4
  91.8 0.8 dynamic-slice_convert_fusion.2
  92.6 10.6 %multiply_reduce_fusion.2 = (f32[128,128]{1,0:T(8,128)S(1)}, f32[128,128]{1,0:T(8,128)S(1)}) fusion(f32[128,128]{1,0:T(8,128)S(1)} %bitcast_convert_fusion.4, f32[128]{0:T(128)S(1)} %get-tuple-element.295, f32[128]{0:T(128)S(1)} %get-tuple-element.248, f32[128]{0:T(128)S(1)} %get-tuple-element.249, f32[128,128]{1,0:T(8,128)S(1)} %bitcast_convert_fusion.5, ...), kind=kLoop, calls=%fused_computation.5.clone.1 | loop fusion | flops 44007424 | bytes 329216 | tf_op jit(solution)/shard_map/while/body/reduce_sum | solution.py:33
  103.9 0.0 copy-start.1
  103.9 0.0 copy-start
  103.9 0.7 copy-done.1
  104.6 0.0 reduce-scatter.3.cloned.1.call-update
  104.6 0.0 reduce-scatter.5.cloned.1.call-start
  104.6 0.6 copy-done
  105.3 0.1 reduce-scatter.5.cloned.1.call-update
  105.3 105.9 %reduce-scatter.3.cloned.1.call-done = f32[96,128]{1,0:T(8,128)} async-done(((f32[384,128]{1,0:T(8,128)}), f32[96,128]{1,0:T(8,128)}) %reduce-scatter.3.cloned.1.call-update) | async-done | bytes 49168 | tf_op jit(solution)/shard_map/reduce_scatter | solution.py:64
  211.2 147.3 %reduce-scatter.5.cloned.1.call-done = f32[1,64,128]{2,1,0:T(8,128)} async-done(((f32[1,4096,128]{2,1,0:T(8,128)}), f32[1,64,128]{2,1,0:T(8,128)}) %reduce-scatter.5.cloned.1.call-update) | async-done | bytes 32784 | tf_op jit(solution)/shard_map/reduce_scatter | solution.py:65
  (10 shorter events, 0.1 us)
Async XLA Ops:
  9.1 40.7 %copy-start.2 = (s32[1,1,8]{2,1,0:T(1,128)S(1)}, s32[1,1,8]{2,1,0:T(1,128)}, u32[]{:S(2)}) copy-start(s32[1,1,8]{2,1,0:T(1,128)} %param.15) | copy-start | bytes 100
  9.1 40.7 %copy-start.3 = (s32[1,1,8]{2,1,0:T(1,128)S(1)}, s32[1,1,8]{2,1,0:T(1,128)}, u32[]{:S(2)}) copy-start(s32[1,1,8]{2,1,0:T(1,128)} %param.16) | copy-start | bytes 100
  9.1 40.7 %copy-start.4 = (f32[128]{0:T(128)S(1)}, f32[128]{0:T(128)}, u32[]{:S(2)}) copy-start(f32[128]{0:T(128)} %param.13) | copy-start | bytes 1540
  9.1 40.4 %all-to-all-start = ((bf16[64,1,64,128]{3,2,1,0:T(8,128)(2,1)}), bf16[64,1,64,128]{3,2,1,0:T(8,128)(2,1)S(1)}, u32[]{:S(2)}, u32[]{:S(2)}) async-start(bf16[64,1,64,128]{3,2,1,0:T(8,128)(2,1)} %stack.2), calls=%async_computation | async-start | bytes 2097152 | tf_op jit(solution)/shard_map/all_to_all | solution.py:13
  21.4 189.9 %reduce-scatter.3.cloned.1.call-start = ((), (), s32[]{:S(2)}) async-start(), calls=%async_computation.3 | async-start | bytes 245760 | tf_op jit(solution)/shard_map/reduce_scatter | solution.py:64
  103.9 0.7 copy-start.1
  103.9 1.4 copy-start
  104.6 253.9 %reduce-scatter.5.cloned.1.call-start = ((), (), s32[]{:S(2)}) async-start(), calls=%async_computation.4 | async-start | bytes 2129920 | tf_op jit(solution)/shard_map/reduce_scatter | solution.py:65
Sparse Core Ops, SparseCore 0:
  104.7 106.4 reduce-scatter.2
  216.4 142.0 reduce-scatter.4
